TPU v7x, 256 devices: a whole 4x4x8 slice. The times are simulated.
256 devices in a mesh: row: 8 (over x, core), cls: 32 (over y, z).
Axes of the slice: x: 4, y: 4, z: 8, core: 2. Of those that a mesh axis runs over, the one named last changes fastest.
Arguments:
- images: bfloat16 [16384, 512], P('row'), may hold values from -6 to 6
- image_index: int32 [8192], P('row'), may hold values from 0 to 16383, as said below
- labels: int32 [8192], P('row'), may hold values from 0 to 21503
- counts: int32 [8192], P('row'), may hold values from 1 to 10
- projection: bfloat16 [2, 512, 512], P(None, None, 'cls'), may hold values from -0.25 to 0.25
- phase_shift: bfloat16 [2, 512], P(None, 'cls'), may hold values from 0 to 6.28125
- predictions: bfloat16 [8192, 21504], P('row', 'cls'), may hold values from -20 to 20
- block_weights: bfloat16 [2, 512, 21504], P(None, None, 'cls'), may hold values from -3 to 3
Outputs:
- updated_weights: float32 [2, 512, 21504], P(None, None, 'cls')
- residual_tiles: float32 [8192, 21504], P('row', 'cls')
- weighted_loss: float32 [], replicated
Inputs may be any that keep to these rules, and one draw needn't show every extreme that they name: `image_index`: row r names one of the 2048 images that begin at (r // 1024) * 2048.
All inputs are finite; a program needn't handle non-finite values.
Results may differ from a plain program's by a relative error of at most 0.0086.
Values may be sent and summed in bfloat16 or wider, within the bound.
No kernel may reach another device: no remote copies, remote signals or barrier semaphores. Data moves between devices by JAX's collectives and lax.ppermute only.
A program may use at most 128 MiB of HBM per device.

v0:
```python
import functools

import jax
import jax.numpy as jnp
from jax import lax
from jax.experimental import pallas as pl
from jax.experimental.pallas import tpu as pltpu
from jax.sharding import Mesh
from jax.sharding import PartitionSpec as P


CLS = ("cls_0", "cls_1")
ROW = ("row_0", "row_1")
X, CORE = ROW

AMPLITUDE = 1.4142135623730951
PENALTY = 0.1
HALF_TURN_COS = (
    0.9999999997801796,
    -4.9348021370964545,
    4.0587091598532785,
    -1.3352120048696623,
    0.23493731750810104,
    -0.024396324505313864,
)
INV_TWO_PI = 0.15915494309189535
NT = (((1,), (1,)), ((), ()))
NN = (((1,), (0,)), ((), ()))
TN = (((0,), (0,)), ((), ()))
FAST_NORM = 12.0
VMEM = pltpu.CompilerParams(vmem_limit_bytes=56 << 20)


def dot(a, b, dims=NN, precision=None):
    return lax.dot_general(a, b, dims, precision=precision, preferred_element_type=jnp.float32)


def exact_dot(a, b, dims):
    return dot(a, b, dims, lax.Precision.HIGHEST)


def split(x):
    high = x.astype(jnp.bfloat16)
    low = (x - high.astype(jnp.float32)).astype(jnp.bfloat16)
    return high, low


def dot3(ah, al, bh, bl):
    return dot(ah, bh) + (dot(ah, bl) + dot(al, bh))


def scaled_cos(turns):
    f = turns - jnp.floor(turns + 0.5)
    z = f * f
    c = z * HALF_TURN_COS[5] + HALF_TURN_COS[4]
    for k in range(3, -1, -1):
        c = c * z + HALF_TURN_COS[k]
    return (2.0 * AMPLITUDE) * (c * c) - AMPLITUDE


def partner(array, axis=CORE, offset=1):
    return lax.ppermute(array, axis, [(i, i ^ offset) for i in range(lax.axis_size(axis))])


def after(array, other):
    return lax.optimization_barrier((array, other))[0]


def everyones(array, axes):
    count = lax.axis_size(axes)
    return lax.all_to_all(jnp.broadcast_to(array[None], (count, *array.shape)), axes, 0, 0, tiled=True)


def summed(array, axes):
    return jnp.sum(everyones(array, axes), axis=0)


def features_kernel(
    place_ref, own_ref, other_ref, picked_ref, counts_ref, feat_ref, weighted_ref, mine_ref, theirs_ref, proj_ref
):
    step = pl.program_id(0)
    slot, core = place_ref[0], place_ref[1]
    fs, din = own_ref.shape[1], picked_ref.shape[1]
    rows = proj_ref.shape[0]
    per = rows // fs
    inner = own_ref.shape[0] // per
    block, group = step // inner, step % inner
    for k in range(per):
        at = group * per + k
        proj_ref[k * fs : (k + 1) * fs, :] = jnp.where(
            block == core, own_ref[at].astype(jnp.float32), other_ref[at].astype(jnp.float32)
        ).astype(jnp.bfloat16)
    mixed = dot(proj_ref[:, 0:din], picked_ref[...], NT)
    phase = proj_ref[:, din : din + 1].astype(jnp.float32)
    feats = scaled_cos(mixed * INV_TWO_PI + phase * INV_TWO_PI).astype(jnp.bfloat16)
    at = pl.ds(pl.multiple_of(step * rows, rows), rows)
    feat_ref[at, :] = feats
    weighted_ref[at, :] = (feats.astype(jnp.float32) * counts_ref[...]).astype(jnp.bfloat16)

    @pl.when(step == pl.num_programs(0) - 1)
    def _():
        half = feat_ref.shape[0] // 2
        part = fs // 2
        first = pl.multiple_of(slot * fs, fs)
        lead = feat_ref[pl.ds(first, fs), :]
        later = feat_ref[pl.ds(pl.multiple_of(half + first, fs), fs), :]
        ones = jnp.ones((16, lead.shape[1]), jnp.bfloat16)
        both = dot(jnp.concatenate([lead, later, ones], axis=0), weighted_ref[...], NT)
        parts = (both[0:fs, 0:half], both[fs : 2 * fs, half:], both[0:fs, half:])
        for k, value in enumerate(parts):
            mine_ref[k] = jnp.where(core == 0, value[0:part], value[part:])
            theirs_ref[k] = jnp.where(core == 0, value[part:], value[0:part])
        row = lax.broadcasted_iota(jnp.int32, (8, half), 0)
        times = jnp.broadcast_to(counts_ref[...], ones.shape).astype(jnp.bfloat16)
        plain = dot(times, feat_ref[...], NT)[0:8]
        rounded = both[2 * fs : 2 * fs + 8]
        sums = jnp.where(row == 0, plain[:, 0:half], plain[:, half:])
        sums = jnp.where(row == 2, rounded[:, 0:half], sums)
        sums = jnp.where(row == 3, rounded[:, half:], sums)
        sums = jnp.where(row == 4, jnp.sum(counts_ref[...]), sums)
        mine_ref[3, 0:8] = sums
        theirs_ref[3, 0:8] = sums


def make_features(place, own, other, picked, counts_row):
    cls, fs, wide = own.shape
    rows, din = picked.shape
    total = 2 * cls * fs
    per = max(1, 256 // fs)
    whole = pl.BlockSpec((cls, fs, wide), lambda i: (0, 0, 0))
    part = pl.BlockSpec((4, fs // 2, total // 2), lambda i: (0, 0, 0))
    feature = pl.BlockSpec((total, rows), lambda i: (0, 0))
    return pl.pallas_call(
        features_kernel,
        grid=(2 * cls // per,),
        in_specs=[
            pl.BlockSpec(memory_space=pltpu.SMEM),
            whole,
            whole,
            pl.BlockSpec((rows, din), lambda i: (0, 0)),
            pl.BlockSpec((1, rows), lambda i: (0, 0)),
        ],
        out_specs=[feature, feature, part, part],
        out_shape=[
            jax.ShapeDtypeStruct((total, rows), jnp.bfloat16),
            jax.ShapeDtypeStruct((total, rows), jnp.bfloat16),
            jax.ShapeDtypeStruct((4, fs // 2, total // 2), jnp.float32),
            jax.ShapeDtypeStruct((4, fs // 2, total // 2), jnp.float32),
        ],
        scratch_shapes=[pltpu.VMEM((per * fs, wide), jnp.bfloat16)],
        compiler_params=VMEM,
        name="features",
    )(place, own, other, picked, counts_row)


def start_residual(start, labels, preds):
    classes = start + lax.broadcasted_iota(jnp.int32, preds.shape, 0)
    return jnp.where(labels == classes, 1.0, 0.0) - preds.astype(jnp.float32)


def corr_kernel(place_ref, weighted_ref, labels_ref, preds_ref, mine_ref, theirs_ref):
    tile = preds_ref.shape[0]
    lanes = mine_ref.shape[2]
    slot, core, x = place_ref[0], place_ref[1], place_ref[2]
    start = slot * (tile * pl.num_programs(0)) + pl.program_id(0) * tile
    residual = start_residual(start, labels_ref[...], preds_ref[...])
    sums = dot(residual.astype(jnp.bfloat16), weighted_ref[...], NT)
    for k in range(mine_ref.shape[0]):
        even = sums[:, 2 * k * lanes : (2 * k + 1) * lanes]
        odd = sums[:, (2 * k + 1) * lanes : (2 * k + 2) * lanes]
        mine_ref[k ^ x] = jnp.where(core == 0, even, odd)
        theirs_ref[k ^ x] = jnp.where(core == 0, odd, even)


def make_corr(place, weighted, labels_row, preds, tiles):
    width, rows = preds.shape
    total = weighted.shape[0]
    tile = width // tiles
    half = jax.ShapeDtypeStruct((4, width, total // 8), jnp.float32)
    half_spec = pl.BlockSpec((4, tile, total // 8), lambda i: (0, i, 0))
    return pl.pallas_call(
        corr_kernel,
        grid=(tiles,),
        in_specs=[
            pl.BlockSpec(memory_space=pltpu.SMEM),
            pl.BlockSpec((total, rows), lambda i: (0, 0)),
            pl.BlockSpec((1, rows), lambda i: (0, 0)),
            pl.BlockSpec((tile, rows), lambda i: (i, 0)),
        ],
        out_specs=[half_spec, half_spec],
        out_shape=[half, half],
        compiler_params=VMEM,
        cost_estimate=pl.CostEstimate(flops=2 * width * rows * total, transcendentals=0, bytes_accessed=8 * width * total),
        name="corr",
    )(place, weighted, labels_row, preds)


def put_together(place_ref, own_ref, other_ref, k):
    core = place_ref[1]
    own, other = own_ref[k], other_ref[k]
    return jnp.where(core == 0, own, other), jnp.where(core == 0, other, own)


def inverse_kernel(place_ref, count_ref, totals_ref, own_ref, other_ref, high_ref, low_ref, a_ref, ah_ref, al_ref, x_ref, *, block):
    n = x_ref.shape[0]
    part = own_ref.shape[1]
    scale = 1.0 / count_ref[0]
    for k in range(own_ref.shape[0]):
        upper, lower = put_together(place_ref, own_ref, other_ref, k)
        x_ref[2 * k * part : (2 * k + 1) * part, :] = upper
        x_ref[(2 * k + 1) * part : (2 * k + 2) * part, :] = lower
    row = lax.broadcasted_iota(jnp.int32, (n, n), 0)
    eye = jnp.where(row == lax.broadcasted_iota(jnp.int32, (n, n), 1), 1.0, 0.0)
    chosen = lax.broadcasted_iota(jnp.int32, totals_ref.shape, 0)
    plain = jnp.where(chosen == 0, totals_ref[block : block + 1, :] * scale, 0.0)
    rounded = jnp.where(chosen == 0, totals_ref[block + 2 : block + 3, :] * scale, 0.0)
    a = (x_ref[...] * scale + PENALTY * eye) - exact_dot(plain, rounded, TN)
    a_ref[...] = a
    ah_ref[...], al_ref[...] = split(a)
    bound = jnp.maximum(jnp.max(jnp.sum(jnp.abs(a), axis=1)), 0.1)
    least = 0.09
    fast = bound <= FAST_NORM

    def stretch(low):
        return 1.96 / (1.0 + low)

    def narrow(low):
        y = low * stretch(low)
        return y * (2.0 - y)

    low = least / bound
    alpha = stretch(low) / bound
    x_ref[...] = (2.0 * alpha) * eye - (alpha * alpha) * a
    low = narrow(low)

    def rough(low):
        y = x_ref[...] * stretch(low)
        yb = y.astype(jnp.bfloat16)
        r = eye - dot(ah_ref[...], yb)
        x_ref[...] = y + dot(yb, r.astype(jnp.bfloat16))
        return narrow(low)

    low = lax.while_loop(lambda low: jnp.logical_and(fast, low < 0.9), rough, low)

    def fine(carry):
        step, _ = carry
        x = x_ref[...]
        xh, xl = split(x)
        r = eye - dot3(ah_ref[...], al_ref[...], xh, xl)
        rb = r.astype(jnp.bfloat16)
        more = r + dot(rb, rb)
        x_ref[...] = x + dot(xh, more.astype(jnp.bfloat16))
        return step + 1, jnp.sum(r * r)

    def careful(carry):
        step, low, _ = carry
        early = low < 0.9
        y = x_ref[...] * jnp.where(early, stretch(low), 1.0)
        r = eye - exact_dot(a_ref[...], y, NN)
        x_ref[...] = y + exact_dot(y, r, NN)
        return step + 1, jnp.where(early, narrow(low), low), jnp.where(early, 1.0, jnp.sum(r * r))

    far = jnp.float32(1.0)
    lax.while_loop(
        lambda carry: jnp.logical_and(carry[0] < 20, carry[1] > 1e-2), fine, (0, jnp.where(fast, far, 0.0))
    )
    lax.while_loop(
        lambda carry: jnp.logical_and(carry[0] < 40, carry[2] > 1e-5), careful, (0, low, jnp.where(fast, 0.0, far))
    )
    x = x_ref[...]
    right = exact_dot(rounded, x, NN)
    left = exact_dot(x, plain, NT)
    weight = 1.0 / (1.0 + jnp.sum(right * plain))
    high_ref[...], low_ref[...] = split(x - exact_dot(left, right * weight, NN))


def make_inverse(place, count, totals, own, other, block):
    cls, part, n = own.shape[0], own.shape[-2], own.shape[-1]
    if own.ndim == 4:
        whole = pl.BlockSpec((cls, None, part, n), lambda i: (0, 0, 0, 0))
    else:
        whole = pl.BlockSpec((cls, part, n), lambda i: (0, 0, 0))
    smem = pl.BlockSpec(memory_space=pltpu.SMEM)
    out = jax.ShapeDtypeStruct((n, n), jnp.bfloat16)
    return pl.pallas_call(
        functools.partial(inverse_kernel, block=block),
        grid=(1,),
        in_specs=[smem, smem, pl.BlockSpec((8, n), lambda i: (0, 0)), whole, whole],
        out_specs=[pl.BlockSpec((n, n), lambda i: (0, 0))] * 2,
        out_shape=[out, out],
        scratch_shapes=[
            pltpu.VMEM((n, n), jnp.float32),
            pltpu.VMEM((n, n), jnp.bfloat16),
            pltpu.VMEM((n, n), jnp.bfloat16),
            pltpu.VMEM((n, n), jnp.float32),
        ],
        compiler_params=VMEM,
        cost_estimate=pl.CostEstimate(flops=40 * 2 * n**3, transcendentals=0, bytes_accessed=12 * n * n),
        name="inverse",
    )(place, count, totals, own, other)


def update_kernel(
    place_ref,
    count_ref,
    corr_own_ref,
    corr_other_ref,
    weights_ref,
    high0_ref,
    low0_ref,
    high1_ref,
    low1_ref,
    cross_own_ref,
    cross_other_ref,
    feat_ref,
    labels_ref,
    preds_ref,
    counts_ref,
    updated_ref,
    residual_ref,
    loss_ref,
    rows_ref,
    cross_high_ref,
    cross_low_ref,
):
    step = pl.program_id(0)
    tile, _ = preds_ref.shape
    slot, core, x = place_ref[0], place_ref[1], place_ref[2]
    start = slot * (tile * pl.num_programs(0)) + step * tile
    scale = 1.0 / count_ref[0]

    @pl.when(step == 0)
    def _():
        for k in range(cross_own_ref.shape[0]):
            rows16 = jnp.concatenate(put_together(place_ref, cross_own_ref, cross_other_ref, k), axis=0)
            fs = rows16.shape[0]
            cross_high_ref[k * fs : (k + 1) * fs, :], cross_low_ref[k * fs : (k + 1) * fs, :] = split(rows16)

    def sums_of(block):
        pieces = []
        for k in (2 * block, 2 * block + 1):
            own, other = corr_own_ref[k ^ x], corr_other_ref[k ^ x]
            pieces.append(jnp.where(core == 0, own, other))
            pieces.append(jnp.where(core == 0, other, own))
        return jnp.concatenate(pieces, axis=1)

    def change_of(block, sums, inv_high, inv_low):
        old = weights_ref[block].astype(jnp.float32)
        high, low = split(sums * scale - PENALTY * old)
        change = dot3(high, low, inv_high, inv_low)
        updated_ref[block] = old + change
        return change.astype(jnp.bfloat16)

    first = change_of(0, sums_of(0), high0_ref[...], low0_ref[...])
    moved = dot(first, cross_high_ref[...]) + dot(first, cross_low_ref[...])
    second = change_of(1, sums_of(1) - moved, high1_ref[...], low1_ref[...])
    residual = start_residual(start, labels_ref[...], preds_ref[...])
    residual = residual - dot(jnp.concatenate([first, second], axis=1), feat_ref[...])
    residual_ref[...] = residual
    squares = jnp.sum(residual * residual, axis=0, keepdims=True)

    @pl.when(step == 0)
    def _():
        rows_ref[...] = squares

    @pl.when(step > 0)
    def _():
        rows_ref[...] += squares

    @pl.when(step == pl.num_programs(0) - 1)
    def _():
        loss = jnp.sum(rows_ref[...] * (counts_ref[...] * scale), axis=1, keepdims=True)
        loss_ref[...] = jnp.broadcast_to(loss, loss_ref.shape)


def make_update(place, count, corr_own, corr_other, weights, inverses, cross_own, cross_other, feats, labels_row, preds, counts_row, tiles):
    width, rows = preds.shape
    total = feats.shape[0]
    n = total // 2
    cls, _, part, _ = cross_own.shape
    tile = width // tiles
    smem = pl.BlockSpec(memory_space=pltpu.SMEM)
    square = pl.BlockSpec((n, n), lambda i: (0, 0))
    sums = pl.BlockSpec((4, tile, total // 8), lambda i: (0, i, 0))
    cross = pl.BlockSpec((cls, None, part, n), lambda i: (0, 1, 0, 0))
    row = pl.BlockSpec((1, rows), lambda i: (0, 0))
    return pl.pallas_call(
        update_kernel,
        grid=(tiles,),
        in_specs=[
            smem,
            smem,
            sums,
            sums,
            pl.BlockSpec((2, tile, n), lambda i: (0, i, 0)),
            square,
            square,
            square,
            square,
            cross,
            cross,
            pl.BlockSpec((total, rows), lambda i: (0, 0)),
            row,
            pl.BlockSpec((tile, rows), lambda i: (i, 0)),
            row,
        ],
        out_specs=[
            pl.BlockSpec((2, tile, n), lambda i: (0, i, 0)),
            pl.BlockSpec((tile, rows), lambda i: (i, 0)),
            pl.BlockSpec((1, 128), lambda i: (0, 0)),
        ],
        out_shape=[
            jax.ShapeDtypeStruct((2, width, n), jnp.float32),
            jax.ShapeDtypeStruct((width, rows), jnp.float32),
            jax.ShapeDtypeStruct((1, 128), jnp.float32),
        ],
        scratch_shapes=[
            pltpu.VMEM((1, rows), jnp.float32),
            pltpu.VMEM((n, n), jnp.bfloat16),
            pltpu.VMEM((n, n), jnp.bfloat16),
        ],
        compiler_params=VMEM,
        name="update",
    )(place, count, corr_own, corr_other, weights, *inverses, cross_own, cross_other, feats, labels_row, preds, counts_row)


def per_device(
    images, image_index, labels, counts, projection, phase_shift, predictions, block_weights
):
    width = predictions.shape[1]
    rows = labels.shape[0]
    classes = width * lax.axis_size(CLS)
    core = lax.axis_index(CORE).astype(jnp.int32)
    place = jnp.stack([lax.axis_index(CLS).astype(jnp.int32), core, lax.axis_index(X).astype(jnp.int32)])

    proj = jnp.pad(
        jnp.concatenate([jnp.transpose(projection, (0, 2, 1)), phase_shift[:, :, None]], axis=2),
        ((0, 0), (0, 0), (0, 127)),
    )
    own_proj = everyones(lax.dynamic_index_in_dim(proj, core, 0, keepdims=False), CLS)
    other_proj = partner(own_proj)

    row_weights = counts.astype(jnp.float32)

    picked = images[image_index % images.shape[0]]
    counts_row = row_weights.reshape(1, rows)
    labels_row = labels.reshape(1, rows)
    preds = predictions.T
    feats, weighted, mine, theirs = make_features(place, own_proj, other_proj, picked, counts_row)

    chip = mine + partner(theirs)
    labels_row = after(labels_row, chip)
    grams = summed(chip, X)
    totals = grams[3, 0:8]
    count = totals[4, 0:1]
    lead_own = everyones(grams[0], CLS)
    lead_other = partner(lead_own)
    rest_own = everyones(after(grams[1:3], lead_other), CLS)
    rest_other = partner(rest_own)

    corr_mine, corr_theirs = make_corr(place, weighted, labels_row, preds, 3)
    halves = after(corr_mine + partner(corr_theirs), grams)
    send = halves.astype(jnp.bfloat16)
    others = range(1, lax.axis_size(X))
    total = halves[0] + sum(partner(send[k], X, k).astype(jnp.float32) for k in others)
    corr_own = jnp.stack([total] + [partner(total, X, k) for k in others])
    corr_other = partner(corr_own)

    lead_inverse = make_inverse(place, count, totals, lead_own, lead_other, 0)
    rest_inverse = make_inverse(place, count, totals, rest_own, rest_other, 1)
    updated, residual, loss = make_update(
        place,
        count,
        corr_own,
        corr_other,
        jnp.transpose(block_weights, (0, 2, 1)),
        [*lead_inverse, *rest_inverse],
        rest_own,
        rest_other,
        feats,
        labels_row,
        preds,
        counts_row,
        3,
    )
    weighted_loss = summed(summed(loss, ROW), CLS)[0, 0] / classes
    return (jnp.transpose(updated, (0, 2, 1)), residual.T, weighted_loss)


def solution(mesh):
    cls = mesh.shape["cls"]
    row = mesh.shape["row"]
    torus = Mesh(
        mesh.devices.reshape(row // 2, 2, max(1, cls // 8), min(8, cls)), ("row_0", "row_1", "cls_0", "cls_1")
    )
    placed = (
        P(ROW, None),
        P(ROW),
        P(ROW),
        P(ROW),
        P(None, None, CLS),
        P(None, CLS),
        P(ROW, CLS),
        P(None, None, CLS),
    )
    return jax.shard_map(
        per_device,
        mesh=torus,
        in_specs=placed,
        out_specs=(P(None, None, CLS), P(ROW, CLS), P()),
        check_vma=False,
    )
```

profile of v0, /device:TPU:2, one launch (start us, length us, event | category | flops | bytes accessed | tf_op | source)
XLA Modules:
  0.0 243.3 jit_solution(3523235441998646241)
XLA Ops:
  2.4 31.4 %all_to_all.30.own_ref = bf16[32,16,640]{2,1,0:T(8,128)(2,1)S(1)} all-to-all(bf16[32,16,640]{2,1,0:T(8,128)(2,1)S(1)} %broadcast_in_dim.24), channel_id=1, replica_groups=mesh['row_0'=4,'row_1'=2,'cls_0'=4,'cls_1'=8] {'cls_0','cls_1'}, dimensions={0} | all-to-all | bytes 1310720 | tf_op jit(solution)/shard_map/all_to_all | solution.py:71
  34.4 5.1 %gather_fusion = bf16[1024,512]{1,0:T(8,128)(2,1)} fusion(bf16[2048,512]{1,0:T(8,128)(2,1)S(1)} %copy-done, s32[1024]{0:T(1024)S(1)} %fusion.5), kind=kCustom, calls=%fused_computation | custom fusion | bytes 2101248 | tf_op jit(solution)/shard_map/gather | solution.py:445
  41.0 9.5 %features.1 = (bf16[1024,1024]{1,0:T(8,128)(2,1)}, bf16[1024,1024]{1,0:T(8,128)(2,1)}, f32[4,8,512]{2,1,0:T(8,128)}, f32[4,8,512]{2,1,0:T(8,128)}) custom-call(s32[3]{0:T(128)} %pad_add_fusion.place_ref, bf16[32,16,640]{2,1,0:T(8,128)(2,1)} %copy-done.3, bf16[32,16,640]{2,1,0:T(8,128)(2,1)} %copy-done.6, bf16[1024,512]{1,0:T(8,128)(2,1)} %gather_fusion, ...), custom_call_target="tpu_custom_call" | custom-call | tf_op jit(solution)/shard_map/features/pallas_call | solution.py:133
  51.0 1.1 collective-permute-done.1
  53.0 10.3 %all_to_all.31 = f32[4,4,8,512]{3,2,1,0:T(8,128)S(1)} all-to-all(f32[4,4,8,512]{3,2,1,0:T(8,128)S(1)} %broadcast_in_dim.51), channel_id=1, replica_groups=mesh['row_0'=4,'row_1'=2,'cls_0'=4,'cls_1'=8] {'row_0'}, dimensions={0} | all-to-all | bytes 524288 | tf_op jit(solution)/shard_map/all_to_all | solution.py:71
  63.4 21.5 %all_to_all.32.own_ref = f32[32,8,512]{2,1,0:T(8,128)S(1)} all-to-all(f32[32,8,512]{2,1,0:T(8,128)S(1)} %broadcast_in_dim.53), channel_id=1, replica_groups=mesh['row_0'=4,'row_1'=2,'cls_0'=4,'cls_1'=8] {'cls_0','cls_1'}, dimensions={0} | all-to-all | bytes 1048576 | tf_op jit(solution)/shard_map/all_to_all | solution.py:71
  84.9 6.0 %corr.1 = (f32[4,672,128]{2,1,0:T(8,128)}, f32[4,672,128]{2,1,0:T(8,128)}) custom-call(s32[3]{0:T(128)} %pad_add_fusion.place_ref, bf16[1024,1024]{1,0:T(8,128)(2,1)} %get-tuple-element.21.weighted_ref, s32[1,1024]{1,0:T(1,128)} %bitcast.45, bf16[672,1024]{1,0:T(8,128)(2,1)} %bitcast.37), custom_call_target="tpu_custom_call" | custom-call | flops 1409286144 | bytes 5505024 | tf_op jit(solution)/shard_map/corr/pallas_call | solution.py:181
  91.2 1.1 broadcast_in_dim.54
  92.4 5.3 %all-to-all-start.3 = ((f32[32,2,8,512]{3,2,1,0:T(8,128)}), f32[32,2,8,512]{3,2,1,0:T(8,128)S(1)}, u32[]{:S(2)}, u32[]{:S(2)}) async-start(f32[32,2,8,512]{3,2,1,0:T(8,128)} %broadcast_in_dim.54), calls=%async_computation.3 | async-start | bytes 2097152 | tf_op jit(solution)/shard_map/all_to_all | solution.py:71
  97.7 1.9 add.39
  99.7 1.5 collective-permute-start.3
  101.8 2.1 collective-permute-start.4
  103.9 2.8 %collective-permute-done.3 = bf16[672,128]{1,0:T(8,128)(2,1)S(1)} collective-permute-done((bf16[672,128]{1,0:T(8,128)(2,1)S(1)}, bf16[672,128]{1,0:T(8,128)(2,1)S(1)}, u32[]{:S(2)}, u32[]{:S(2)}) %collective-permute-start.3) | collective-permute-done | bytes 172064 | tf_op jit(solution)/shard_map/ppermute | solution.py:62
  106.7 4.2 %collective-permute-done.5 = bf16[672,128]{1,0:T(8,128)(2,1)S(1)} collective-permute-done((bf16[672,128]{1,0:T(8,128)(2,1)S(1)}, bf16[672,128]{1,0:T(8,128)(2,1)S(1)}, u32[]{:S(2)}, u32[]{:S(2)}) %collective-permute-start.5) | collective-permute-done | bytes 172064 | tf_op jit(solution)/shard_map/ppermute | solution.py:62
  111.6 3.3 %collective-permute-start.7 = (f32[672,128]{1,0:T(8,128)S(1)}, f32[672,128]{1,0:T(8,128)}, u32[]{:S(2)}, u32[]{:S(2)}) collective-permute-start(f32[672,128]{1,0:T(8,128)S(1)} %bitcast_add_fusion), channel_id=1, source_target_pairs={{0,128},{64,192},{128,0},{192,64},{1,129},{65,193},{129,1},{193,65... | collective-permute-start | bytes 1032200 | tf_op jit(solution)/shard_map/ppermute | solution.py:62
  115.7 11.0 %all-to-all-done.3.own_ref.cross_own_ref = f32[32,2,8,512]{3,2,1,0:T(8,128)S(1)} async-done(((f32[32,2,8,512]{3,2,1,0:T(8,128)}), f32[32,2,8,512]{3,2,1,0:T(8,128)S(1)}, u32[]{:S(2)}, u32[]{:S(2)}) %all-to-all-start.3) | async-done | bytes 1048608 | tf_op jit(solution)/shard_map/all_to_all | solution.py:71
  127.3 1.8 collective-permute-done.6
  129.1 1.3 pad_maximum_fusion.corr_own_ref
  130.7 35.0 %inverse.2 = (bf16[512,512]{1,0:T(8,128)(2,1)}, bf16[512,512]{1,0:T(8,128)(2,1)}) custom-call(s32[3]{0:T(128)} %pad_add_fusion.place_ref, f32[1]{0:T(128)} %bitcast.8.count_ref, f32[8,512]{1,0:T(8,128)} %copy-done.8, f32[32,8,512]{2,1,0:T(8,128)} %copy-done.7, f32[32,8,512]{2,1,0:T(8,128)} %copy-done.11), custom_call_target="tpu_custom_call" | custom-call | flops 10737418240 | bytes 3145728 | tf_op jit(solution)/shard_map/inverse/pallas_call | solution.py:285
  166.7 35.3 %inverse.3 = (bf16[512,512]{1,0:T(8,128)(2,1)}, bf16[512,512]{1,0:T(8,128)(2,1)}) custom-call(s32[3]{0:T(128)} %pad_add_fusion.place_ref, f32[1]{0:T(128)} %bitcast.8.count_ref, f32[8,512]{1,0:T(8,128)} %copy-done.8, f32[32,2,8,512]{3,2,1,0:T(8,128)} %copy-done.2, f32[32,2,8,512]{3,2,1,0:T(8,128)} %copy-done.5), custom_call_target="tpu_custom_call" | custom-call | flops 10737418240 | bytes 3145728 | tf_op jit(solution)/shard_map/inverse/pallas_call | solution.py:285
  202.0 1.1 copy-done.4
  203.1 11.3 %update.1 = (f32[2,672,512]{2,1,0:T(8,128)}, f32[672,1024]{1,0:T(8,128)}, f32[1,128]{1,0:T(1,128)}) custom-call(s32[3]{0:T(128)} %pad_add_fusion.place_ref, f32[1]{0:T(128)} %bitcast.8.count_ref, f32[4,672,128]{2,1,0:T(8,128)} %copy-done.1, f32[4,672,128]{2,1,0:T(8,128)} %copy-done.4, bf16[2,672,512]{2,1,0:T(8,128)(2,1)} %bitcast.39, ...), custom_call_target="tpu_custom_call" | custom-call | tf_op jit(solution)/shard_map/update/pallas_call | solution.py:387
  215.1 8.2 %all_to_all.33 = f32[8,1,128]{2,1,0:T(1,128)S(1)} all-to-all(f32[8,1,128]{2,1,0:T(1,128)S(1)} %broadcast_in_dim.56), channel_id=1, replica_groups=mesh['row_0'=4,'row_1'=2,'cls_0'=4,'cls_1'=8] {'row_0','row_1'}, dimensions={0} | all-to-all | bytes 8192 | tf_op jit(solution)/shard_map/all_to_all | solution.py:71
  223.3 18.8 %all_to_all.34 = f32[32,1,128]{2,1,0:T(1,128)S(1)} all-to-all(f32[32,1,128]{2,1,0:T(1,128)S(1)} %broadcast_in_dim.57), channel_id=1, replica_groups=mesh['row_0'=4,'row_1'=2,'cls_0'=4,'cls_1'=8] {'cls_0','cls_1'}, dimensions={0} | all-to-all | bytes 32768 | tf_op jit(solution)/shard_map/all_to_all | solution.py:71
  (60 shorter events, 10.5 us)
Async XLA Ops:
  0.6 33.8 %copy-start = (bf16[2048,512]{1,0:T(8,128)(2,1)S(1)}, bf16[2048,512]{1,0:T(8,128)(2,1)}, u32[]{:S(2)}) copy-start(bf16[2048,512]{1,0:T(8,128)(2,1)} %param.8) | copy-start | bytes 6291460
  0.6 33.2 %copy-start.9 = (s32[1024]{0:T(1024)S(1)}, s32[1024]{0:T(1024)}, u32[]{:S(2)}) copy-start(s32[1024]{0:T(1024)} %param.11) | copy-start | bytes 12292
  0.7 33.8 %copy-start.10 = (s32[1024]{0:T(1024)S(1)}, s32[1024]{0:T(1024)}, u32[]{:S(2)}) copy-start(s32[1024]{0:T(1024)} %param.9) | copy-start | bytes 12292
  33.8 5.7 %copy-start.3 = (bf16[32,16,640]{2,1,0:T(8,128)(2,1)}, bf16[32,16,640]{2,1,0:T(8,128)(2,1)S(1)}, u32[]{:S(2)}) copy-start(bf16[32,16,640]{2,1,0:T(8,128)(2,1)S(1)} %all_to_all.30.own_ref) | copy-start | bytes 1966084
  33.8 6.4 %collective-permute-start = (bf16[32,16,640]{2,1,0:T(8,128)(2,1)S(1)}, bf16[32,16,640]{2,1,0:T(8,128)(2,1)S(1)}, u32[]{:S(2)}, u32[]{:S(2)}) collective-permute-start(bf16[32,16,640]{2,1,0:T(8,128)(2,1)S(1)} %all_to_all.30.own_ref), channel_id=1, source_target_pairs={{0,32},{32,0},{1,33},{33,1},{2,34},{34,2},{3,35},{35,3},{4,36},{36... | collective-permute-start | bytes 1966088 | tf_op jit(solution)/shard_map/ppermute | solution.py:62
  50.5 1.6 collective-permute-start.1
  63.4 51.8 %copy-start.8 = (f32[8,512]{1,0:T(8,128)}, f32[8,512]{1,0:T(8,128)S(1)}, u32[]{:S(2)}) copy-start(f32[8,512]{1,0:T(8,128)S(1)} %get-tuple-element.39.totals_ref) | copy-start | bytes 49156
  84.9 6.0 %copy-start.7 = (f32[32,8,512]{2,1,0:T(8,128)}, f32[32,8,512]{2,1,0:T(8,128)S(1)}, u32[]{:S(2)}) copy-start(f32[32,8,512]{2,1,0:T(8,128)S(1)} %all_to_all.32.own_ref) | copy-start | bytes 1572868
  84.9 6.3 %collective-permute-start.10 = (f32[32,8,512]{2,1,0:T(8,128)S(1)}, f32[32,8,512]{2,1,0:T(8,128)S(1)}, u32[]{:S(2)}, u32[]{:S(2)}) collective-permute-start(f32[32,8,512]{2,1,0:T(8,128)S(1)} %all_to_all.32.own_ref), channel_id=1, source_target_pairs={{0,32},{32,0},{1,33},{33,1},{2,34},{34,2},{3,35},{35,3},{4,36},{36... | collective-permute-start | bytes 1572872 | tf_op jit(solution)/shard_map/ppermute | solution.py:62
  90.9 6.8 %collective-permute-start.2 = (f32[4,672,128]{2,1,0:T(8,128)}, f32[4,672,128]{2,1,0:T(8,128)}, u32[]{:S(2)}, u32[]{:S(2)}) collective-permute-start(f32[4,672,128]{2,1,0:T(8,128)} %get-tuple-element.24), channel_id=1, source_target_pairs={{0,32},{32,0},{1,33},{33,1},{2,34},{34,2},{3,35},{35,3},{4,36},{36... | collective-permute-start | bytes 4128776 | tf_op jit(solution)/shard_map/ppermute | solution.py:62
  91.2 1.1 copy-start.11
  92.4 34.3 %all-to-all-start.3 = ((f32[32,2,8,512]{3,2,1,0:T(8,128)}), f32[32,2,8,512]{3,2,1,0:T(8,128)S(1)}, u32[]{:S(2)}, u32[]{:S(2)}) async-start(f32[32,2,8,512]{3,2,1,0:T(8,128)} %broadcast_in_dim.54), calls=%async_computation.3 | async-start | bytes 2097152 | tf_op jit(solution)/shard_map/all_to_all | solution.py:71
  99.7 7.0 %collective-permute-start.3 = (bf16[672,128]{1,0:T(8,128)(2,1)S(1)}, bf16[672,128]{1,0:T(8,128)(2,1)S(1)}, u32[]{:S(2)}, u32[]{:S(2)}) collective-permute-start(bf16[672,128]{1,0:T(8,128)(2,1)S(1)} %get-tuple-element.35), channel_id=1, source_target_pairs={{0,64},{64,0},{128,192},{192,128},{1,65},{65,1},{129,193},{193,129... | collective-permute-start | bytes 516104 | tf_op jit(solution)/shard_map/ppermute | solution.py:62
  101.3 9.6 %collective-permute-start.5 = (bf16[672,128]{1,0:T(8,128)(2,1)S(1)}, bf16[672,128]{1,0:T(8,128)(2,1)S(1)}, u32[]{:S(2)}, u32[]{:S(2)}) collective-permute-start(bf16[672,128]{1,0:T(8,128)(2,1)S(1)} %get-tuple-element.36), channel_id=1, source_target_pairs={{0,192},{64,128},{128,64},{192,0},{1,193},{65,129},{129,65},{193,1... | collective-permute-start | bytes 516104 | tf_op jit(solution)/shard_map/ppermute | solution.py:62
  101.8 9.0 %collective-permute-start.4 = (bf16[672,128]{1,0:T(8,128)(2,1)S(1)}, bf16[672,128]{1,0:T(8,128)(2,1)S(1)}, u32[]{:S(2)}, u32[]{:S(2)}) collective-permute-start(bf16[672,128]{1,0:T(8,128)(2,1)S(1)} %get-tuple-element.37), channel_id=1, source_target_pairs={{0,128},{64,192},{128,0},{192,64},{1,129},{65,193},{129,1},{193,65... | collective-permute-start | bytes 516104 | tf_op jit(solution)/shard_map/ppermute | solution.py:62
  111.0 16.3 %collective-permute-start.8 = (f32[672,128]{1,0:T(8,128)S(1)}, f32[672,128]{1,0:T(8,128)}, u32[]{:S(2)}, u32[]{:S(2)}) collective-permute-start(f32[672,128]{1,0:T(8,128)S(1)} %bitcast_add_fusion), channel_id=1, source_target_pairs={{0,192},{64,128},{128,64},{192,0},{1,193},{65,129},{129,65},{193,1... | collective-permute-start | bytes 1032200 | tf_op jit(solution)/shard_map/ppermute | solution.py:62
  111.6 15.7 %collective-permute-start.7 = (f32[672,128]{1,0:T(8,128)S(1)}, f32[672,128]{1,0:T(8,128)}, u32[]{:S(2)}, u32[]{:S(2)}) collective-permute-start(f32[672,128]{1,0:T(8,128)S(1)} %bitcast_add_fusion), channel_id=1, source_target_pairs={{0,128},{64,192},{128,0},{192,64},{1,129},{65,193},{129,1},{193,65... | collective-permute-start | bytes 1032200 | tf_op jit(solution)/shard_map/ppermute | solution.py:62
  114.9 14.2 %collective-permute-start.6 = (f32[672,128]{1,0:T(8,128)S(1)}, f32[672,128]{1,0:T(8,128)}, u32[]{:S(2)}, u32[]{:S(2)}) collective-permute-start(f32[672,128]{1,0:T(8,128)S(1)} %bitcast_add_fusion), channel_id=1, source_target_pairs={{0,64},{64,0},{128,192},{192,128},{1,65},{65,1},{129,193},{193,129... | collective-permute-start | bytes 1032200 | tf_op jit(solution)/shard_map/ppermute | solution.py:62
  126.6 3.7 %copy-start.2 = (f32[32,2,8,512]{3,2,1,0:T(8,128)}, f32[32,2,8,512]{3,2,1,0:T(8,128)S(1)}, u32[]{:S(2)}) copy-start(f32[32,2,8,512]{3,2,1,0:T(8,128)S(1)} %all-to-all-done.3.own_ref.cross_own_ref) | copy-start | bytes 3145732
  126.6 39.1 %collective-permute-start.11 = (f32[32,2,8,512]{3,2,1,0:T(8,128)S(1)}, f32[32,2,8,512]{3,2,1,0:T(8,128)S(1)}, u32[]{:S(2)}, u32[]{:S(2)}) collective-permute-start(f32[32,2,8,512]{3,2,1,0:T(8,128)S(1)} %all-to-all-done.3.own_ref.cross_own_ref), channel_id=1, source_target_pairs={{0,32},{32,0},{1,33},{33,1},{2,34},{34,2},{3,35},{35,3},{4,36},{36... | collective-permute-start | bytes 3145736 | tf_op jit(solution)/shard_map/ppermute | solution.py:62
  130.4 35.3 %copy-start.1 = (f32[4,672,128]{2,1,0:T(8,128)}, f32[4,672,128]{2,1,0:T(8,128)S(1)}, u32[]{:S(2)}) copy-start(f32[4,672,128]{2,1,0:T(8,128)S(1)} %pad_maximum_fusion.corr_own_ref) | copy-start | bytes 4128772
  130.4 71.6 %collective-permute-start.9 = (f32[4,672,128]{2,1,0:T(8,128)S(1)}, f32[4,672,128]{2,1,0:T(8,128)S(1)}, u32[]{:S(2)}, u32[]{:S(2)}) collective-permute-start(f32[4,672,128]{2,1,0:T(8,128)S(1)} %pad_maximum_fusion.corr_own_ref), channel_id=1, source_target_pairs={{0,32},{32,0},{1,33},{33,1},{2,34},{34,2},{3,35},{35,3},{4,36},{36... | collective-permute-start | bytes 4128776 | tf_op jit(solution)/shard_map/ppermute | solution.py:62
  165.7 1.0 copy-start.5
  202.0 1.1 copy-start.4
  (1 other events, 0.8 us)
where the time goes:
time: 244 us; the launch traced here: 243 us
  Pallas kernels  97 us (40%)
  blocking collectives  90.3 us (37%)
  waiting for transfers between devices  21.5 us (9%)
  starting transfers between devices  14.8 us (6%)
  local copies, waits for them, and re-layouts  11.5 us (5%)
  other arithmetic  6.26 us (3%)
    all_to_all x5, blocking collectives, everyones(): lax.all_to_all(jnp.broadcast_to(array[None], (count, *array.shape)), axes...  90.3 us
    pallas_call x2, Pallas kernels, make_inverse(): pl.pallas_call(functools.partial(inverse_kernel, block=block), grid=(1,),...  70.3 us
    pallas_call x1, Pallas kernels, make_update(): pl.pallas_call(update_kernel, grid=(tiles,), in_specs=[smem, smem, sums,...  11.3 us
    all_to_all x1, waiting for transfers between devices, everyones(): lax.all_to_all(jnp.broadcast_to(array[None], (count, *array.shape)), axes...  11 us
    ppermute x12, waiting for transfers between devices, partner(): lax.ppermute(array, axis, [(i, i ^ offset) for i in range(lax.axis_size(a...  10.5 us
    pallas_call x1, Pallas kernels, make_features(): pl.pallas_call(features_kernel, grid=(2 * cls // per,), in_specs=[pl.Bloc...  9.47 us
    ppermute x12, starting transfers between devices, partner(): lax.ppermute(array, axis, [(i, i ^ offset) for i in range(lax.axis_size(a...  9.47 us
    pallas_call x1, Pallas kernels, make_corr(): pl.pallas_call(corr_kernel, grid=(tiles,), in_specs=[pl.BlockSpec(memory_...  5.95 us
  transfers between devices with their start and end apart: 13, of which 6 were waited for; matrix products, arithmetic and copies ran while one was open for 5% of the time, Pallas kernels for 31%

commit v1 on v0

--- a/solution.py
+++ b/solution.py
@@ -12,6 +12,7 @@
 CLS = ("cls_0", "cls_1")
 ROW = ("row_0", "row_1")
 X, CORE = ROW
+Y, Z = CLS
 
 AMPLITUDE = 1.4142135623730951
 PENALTY = 0.1
@@ -26,7 +27,6 @@
 INV_TWO_PI = 0.15915494309189535
 NT = (((1,), (1,)), ((), ()))
 NN = (((1,), (0,)), ((), ()))
-TN = (((0,), (0,)), ((), ()))
 FAST_NORM = 12.0
 VMEM = pltpu.CompilerParams(vmem_limit_bytes=56 << 20)
 
@@ -211,10 +211,11 @@
         x_ref[(2 * k + 1) * part : (2 * k + 2) * part, :] = lower
     row = lax.broadcasted_iota(jnp.int32, (n, n), 0)
     eye = jnp.where(row == lax.broadcasted_iota(jnp.int32, (n, n), 1), 1.0, 0.0)
-    chosen = lax.broadcasted_iota(jnp.int32, totals_ref.shape, 0)
-    plain = jnp.where(chosen == 0, totals_ref[block : block + 1, :] * scale, 0.0)
-    rounded = jnp.where(chosen == 0, totals_ref[block + 2 : block + 3, :] * scale, 0.0)
-    a = (x_ref[...] * scale + PENALTY * eye) - exact_dot(plain, rounded, TN)
+    plain = totals_ref[block : block + 1, :] * scale
+    rounded = totals_ref[block + 2 : block + 3, :] * scale
+    plain_column = jnp.sum(eye * plain, axis=1, keepdims=True)
+    rounded_column = jnp.sum(eye * rounded, axis=1, keepdims=True)
+    a = (x_ref[...] * scale + PENALTY * eye) - plain_column * rounded
     a_ref[...] = a
     ah_ref[...], al_ref[...] = split(a)
     bound = jnp.maximum(jnp.max(jnp.sum(jnp.abs(a), axis=1)), 0.1)
@@ -268,10 +269,10 @@
         lambda carry: jnp.logical_and(carry[0] < 40, carry[2] > 1e-5), careful, (0, low, jnp.where(fast, 0.0, far))
     )
     x = x_ref[...]
-    right = exact_dot(rounded, x, NN)
-    left = exact_dot(x, plain, NT)
+    right = jnp.sum(x * rounded_column, axis=0, keepdims=True)
+    left = jnp.sum(x * plain, axis=1, keepdims=True)
     weight = 1.0 / (1.0 + jnp.sum(right * plain))
-    high_ref[...], low_ref[...] = split(x - exact_dot(left, right * weight, NN))
+    high_ref[...], low_ref[...] = split(x - left * (right * weight))
 
 
 def make_inverse(place, count, totals, own, other, block):
@@ -437,7 +438,9 @@
         jnp.concatenate([jnp.transpose(projection, (0, 2, 1)), phase_shift[:, :, None]], axis=2),
         ((0, 0), (0, 0), (0, 127)),
     )
-    own_proj = everyones(lax.dynamic_index_in_dim(proj, core, 0, keepdims=False), CLS)
+    along = everyones(lax.dynamic_index_in_dim(proj, core, 0, keepdims=False), Z)
+    own_proj = everyones(along, Y)
+    own_proj = own_proj.reshape(-1, *own_proj.shape[2:])
     other_proj = partner(own_proj)
 
     row_weights = counts.astype(jnp.float32)
@@ -460,9 +463,8 @@
 
     corr_mine, corr_theirs = make_corr(place, weighted, labels_row, preds, 3)
     halves = after(corr_mine + partner(corr_theirs), grams)
-    send = halves.astype(jnp.bfloat16)
     others = range(1, lax.axis_size(X))
-    total = halves[0] + sum(partner(send[k], X, k).astype(jnp.float32) for k in others)
+    total = halves[0] + sum(partner(halves[k], X, k) for k in others)
     corr_own = jnp.stack([total] + [partner(total, X, k) for k in others])
     corr_other = partner(corr_own)
 
@@ -483,7 +485,7 @@
         counts_row,
         3,
     )
-    weighted_loss = summed(summed(loss, ROW), CLS)[0, 0] / classes
+    weighted_loss = summed(summed(summed(loss, ROW), Z), Y)[0, 0] / classes
     return (jnp.transpose(updated, (0, 2, 1)), residual.T, weighted_loss)
 
 

time: 244 us -> 244 us (level)
  waiting for transfers between devices: 21.5 us -> 41.8 us
  blocking collectives: 90.3 us -> 73.5 us
  Pallas kernels: 97 us -> 88.6 us
  starting transfers between devices: 14.8 us -> 19.2 us
    ppermute x12, waiting for transfers between devices: 10.5 us -> 27.4 us  [partner(): lax.ppermute(array, axis, [(i, i ^ offset) for i in range(lax.axis_size(a...]
    all_to_all x5 -> x6, blocking collectives: 90.3 us -> 73.5 us  [everyones(): lax.all_to_all(jnp.broadcast_to(array[None], (count, *array.shape)), axes...]
    pallas_call x2, Pallas kernels: 70.3 us -> 62 us  [make_inverse(): pl.pallas_call(functools.partial(inverse_kernel, block=block), grid=(1,),...]
    all_to_all x1 -> x2, starting transfers between devices: 5.33 us -> 9.51 us  [everyones(): lax.all_to_all(jnp.broadcast_to(array[None], (count, *array.shape)), axes...]
    all_to_all x1 -> x2, waiting for transfers between devices: 11 us -> 14.4 us  [everyones(): lax.all_to_all(jnp.broadcast_to(array[None], (count, *array.shape)), axes...]
  transfers between devices with their start and end apart: 13 -> 14, of which waited for: 6 -> 8; matrix products, arithmetic and copies ran while one was open for 5% -> 5% of each run, Pallas kernels for 31% -> 28%
where the time goes in v1:
time: 244 us
  Pallas kernels  88.6 us (36%)
  blocking collectives  73.5 us (30%)
  waiting for transfers between devices  41.8 us (17%)
  starting transfers between devices  19.2 us (8%)
  local copies, waits for them, and re-layouts  12.3 us (5%)
  other arithmetic  6.19 us (3%)
    all_to_all x6, blocking collectives, everyones(): lax.all_to_all(jnp.broadcast_to(array[None], (count, *array.shape)), axes...  73.5 us
    pallas_call x2, Pallas kernels, make_inverse(): pl.pallas_call(functools.partial(inverse_kernel, block=block), grid=(1,),...  62 us
    ppermute x12, waiting for transfers between devices, partner(): lax.ppermute(array, axis, [(i, i ^ offset) for i in range(lax.axis_size(a...  27.4 us
    all_to_all x2, waiting for transfers between devices, everyones(): lax.all_to_all(jnp.broadcast_to(array[None], (count, *array.shape)), axes...  14.4 us
    pallas_call x1, Pallas kernels, make_update(): pl.pallas_call(update_kernel, grid=(tiles,), in_specs=[smem, smem, sums,...  11.3 us
    ppermute x12, starting transfers between devices, partner(): lax.ppermute(array, axis, [(i, i ^ offset) for i in range(lax.axis_size(a...  9.69 us
    all_to_all x2, starting transfers between devices, everyones(): lax.all_to_all(jnp.broadcast_to(array[None], (count, *array.shape)), axes...  9.51 us
    pallas_call x1, Pallas kernels, make_features(): pl.pallas_call(features_kernel, grid=(2 * cls // per,), in_specs=[pl.Bloc...  9.45 us
  transfers between devices with their start and end apart: 14, of which 8 were waited for; matrix products, arithmetic and copies ran while one was open for 5% of the time, Pallas kernels for 28%

profile of v1, /device:TPU:2, one launch (start us, length us, event | category | flops | bytes accessed | tf_op | source)
XLA Modules:
  0.0 243.5 jit_solution(15526342966024442955)
XLA Ops:
  2.3 18.0 %all_to_all.40 = bf16[8,16,640]{2,1,0:T(8,128)(2,1)S(1)} all-to-all(bf16[8,16,640]{2,1,0:T(8,128)(2,1)S(1)} %broadcast_in_dim.28), channel_id=1, replica_groups=mesh['row_0'=4,'row_1'=2,'cls_0'=4,'cls_1'=8] {'cls_1'}, dimensions={0} | all-to-all | bytes 327680 | tf_op jit(solution)/shard_map/all_to_all | solution.py:71
  20.4 13.3 %all_to_all.41 = bf16[4,8,16,640]{3,2,1,0:T(8,128)(2,1)S(1)} all-to-all(bf16[4,8,16,640]{3,2,1,0:T(8,128)(2,1)S(1)} %broadcast_in_dim.29), channel_id=1, replica_groups=mesh['row_0'=4,'row_1'=2,'cls_0'=4,'cls_1'=8] {'cls_0'}, dimensions={0} | all-to-all | bytes 1310720 | tf_op jit(solution)/shard_map/all_to_all | solution.py:71
  34.4 5.1 %gather_fusion = bf16[1024,512]{1,0:T(8,128)(2,1)} fusion(bf16[2048,512]{1,0:T(8,128)(2,1)S(1)} %copy-done, s32[1024]{0:T(1024)S(1)} %fusion.5), kind=kCustom, calls=%fused_computation | custom fusion | bytes 2101248 | tf_op jit(solution)/shard_map/gather | solution.py:448
  41.0 9.5 %features.1 = (bf16[1024,1024]{1,0:T(8,128)(2,1)}, bf16[1024,1024]{1,0:T(8,128)(2,1)}, f32[4,8,512]{2,1,0:T(8,128)}, f32[4,8,512]{2,1,0:T(8,128)}) custom-call(s32[3]{0:T(128)} %pad_add_fusion.place_ref, bf16[32,16,640]{2,1,0:T(8,128)(2,1)} %bitcast.39, bf16[32,16,640]{2,1,0:T(8,128)(2,1)} %copy-done.6, bf16[1024,512]{1,0:T(8,128)(2,1)} %gather_fusion, ...), custom_call_target="tpu_custom_call" | custom-call | tf_op jit(solution)/shard_map/features/pallas_call | solution.py:133
  52.9 10.4 %all_to_all.42 = f32[4,4,8,512]{3,2,1,0:T(8,128)S(1)} all-to-all(f32[4,4,8,512]{3,2,1,0:T(8,128)S(1)} %broadcast_in_dim.31), channel_id=1, replica_groups=mesh['row_0'=4,'row_1'=2,'cls_0'=4,'cls_1'=8] {'row_0'}, dimensions={0} | all-to-all | bytes 524288 | tf_op jit(solution)/shard_map/all_to_all | solution.py:71
  64.1 3.9 %all-to-all-start.3 = ((f32[32,8,512]{2,1,0:T(8,128)}), f32[32,8,512]{2,1,0:T(8,128)S(1)}, u32[]{:S(2)}, u32[]{:S(2)}) async-start(f32[32,8,512]{2,1,0:T(8,128)} %broadcast_in_dim.66), calls=%async_computation.3 | async-start | bytes 1048576 | tf_op jit(solution)/shard_map/all_to_all | solution.py:71
  68.0 5.8 %corr.1 = (f32[4,672,128]{2,1,0:T(8,128)}, f32[4,672,128]{2,1,0:T(8,128)}) custom-call(s32[3]{0:T(128)} %pad_add_fusion.place_ref, bf16[1024,1024]{1,0:T(8,128)(2,1)} %get-tuple-element.21.weighted_ref, s32[1,1024]{1,0:T(1,128)} %bitcast.50, bf16[672,1024]{1,0:T(8,128)(2,1)} %bitcast.41), custom_call_target="tpu_custom_call" | custom-call | flops 1409286144 | bytes 5505024 | tf_op jit(solution)/shard_map/corr/pallas_call | solution.py:181
  73.9 10.7 %all-to-all-done.3.own_ref = f32[32,8,512]{2,1,0:T(8,128)S(1)} async-done(((f32[32,8,512]{2,1,0:T(8,128)}), f32[32,8,512]{2,1,0:T(8,128)S(1)}, u32[]{:S(2)}, u32[]{:S(2)}) %all-to-all-start.3) | async-done | bytes 524320 | tf_op jit(solution)/shard_map/all_to_all | solution.py:71
  84.6 1.9 collective-permute-done.10.other_ref
  87.6 5.6 %all-to-all-start.4 = ((f32[32,2,8,512]{3,2,1,0:T(8,128)}), f32[32,2,8,512]{3,2,1,0:T(8,128)S(1)}, u32[]{:S(2)}, u32[]{:S(2)}) async-start(f32[32,2,8,512]{3,2,1,0:T(8,128)} %broadcast_in_dim.67), calls=%async_computation.4 | async-start | bytes 2097152 | tf_op jit(solution)/shard_map/all_to_all | solution.py:71
  93.3 1.9 add.39
  98.2 1.8 collective-permute-start.3
  100.0 7.7 %collective-permute-done.4 = f32[672,128]{1,0:T(8,128)S(1)} collective-permute-done((f32[672,128]{1,0:T(8,128)S(1)}, f32[672,128]{1,0:T(8,128)S(1)}, u32[]{:S(2)}, u32[]{:S(2)}) %collective-permute-start.4) | collective-permute-done | bytes 344096 | tf_op jit(solution)/shard_map/ppermute | solution.py:62
  107.8 5.9 %collective-permute-done.5 = f32[672,128]{1,0:T(8,128)S(1)} collective-permute-done((f32[672,128]{1,0:T(8,128)S(1)}, f32[672,128]{1,0:T(8,128)S(1)}, u32[]{:S(2)}, u32[]{:S(2)}) %collective-permute-start.5) | collective-permute-done | bytes 344096 | tf_op jit(solution)/shard_map/ppermute | solution.py:62
  114.8 2.8 %collective-permute-start.7 = (f32[672,128]{1,0:T(8,128)S(1)}, f32[672,128]{1,0:T(8,128)}, u32[]{:S(2)}, u32[]{:S(2)}) collective-permute-start(f32[672,128]{1,0:T(8,128)S(1)} %bitcast_add_fusion), channel_id=1, source_target_pairs={{0,128},{64,192},{128,0},{192,64},{1,129},{65,193},{129,1},{193,65... | collective-permute-start | bytes 1032200 | tf_op jit(solution)/shard_map/ppermute | solution.py:62
  118.5 3.7 %all-to-all-done.4.own_ref.cross_own_ref = f32[32,2,8,512]{3,2,1,0:T(8,128)S(1)} async-done(((f32[32,2,8,512]{3,2,1,0:T(8,128)}), f32[32,2,8,512]{3,2,1,0:T(8,128)S(1)}, u32[]{:S(2)}, u32[]{:S(2)}) %all-to-all-start.4) | async-done | bytes 1048608 | tf_op jit(solution)/shard_map/all_to_all | solution.py:71
  122.1 8.8 %collective-permute-done.8 = f32[672,128]{1,0:T(8,128)} collective-permute-done((f32[672,128]{1,0:T(8,128)S(1)}, f32[672,128]{1,0:T(8,128)}, u32[]{:S(2)}, u32[]{:S(2)}) %collective-permute-start.8) | collective-permute-done | bytes 344096 | tf_op jit(solution)/shard_map/ppermute | solution.py:62
  131.0 1.8 collective-permute-done.6
  134.4 30.9 %inverse.2 = (bf16[512,512]{1,0:T(8,128)(2,1)}, bf16[512,512]{1,0:T(8,128)(2,1)}) custom-call(s32[3]{0:T(128)} %pad_add_fusion.place_ref, f32[1]{0:T(128)} %bitcast.9.count_ref, f32[8,512]{1,0:T(8,128)} %copy-done.8, f32[32,8,512]{2,1,0:T(8,128)} %copy-done.7, f32[32,8,512]{2,1,0:T(8,128)} %copy-done.11), custom_call_target="tpu_custom_call" | custom-call | flops 10737418240 | bytes 3145728 | tf_op jit(solution)/shard_map/inverse/pallas_call | solution.py:286
  166.3 31.2 %inverse.3 = (bf16[512,512]{1,0:T(8,128)(2,1)}, bf16[512,512]{1,0:T(8,128)(2,1)}) custom-call(s32[3]{0:T(128)} %pad_add_fusion.place_ref, f32[1]{0:T(128)} %bitcast.9.count_ref, f32[8,512]{1,0:T(8,128)} %copy-done.8, f32[32,2,8,512]{3,2,1,0:T(8,128)} %copy-done.2, f32[32,2,8,512]{3,2,1,0:T(8,128)} %copy-done.5), custom_call_target="tpu_custom_call" | custom-call | flops 10737418240 | bytes 3145728 | tf_op jit(solution)/shard_map/inverse/pallas_call | solution.py:286
  198.6 11.3 %update.1 = (f32[2,672,512]{2,1,0:T(8,128)}, f32[672,1024]{1,0:T(8,128)}, f32[1,128]{1,0:T(1,128)}) custom-call(s32[3]{0:T(128)} %pad_add_fusion.place_ref, f32[1]{0:T(128)} %bitcast.9.count_ref, f32[4,672,128]{2,1,0:T(8,128)} %copy-done.1, f32[4,672,128]{2,1,0:T(8,128)} %copy-done.4, bf16[2,672,512]{2,1,0:T(8,128)(2,1)} %bitcast.43, ...), custom_call_target="tpu_custom_call" | custom-call | tf_op jit(solution)/shard_map/update/pallas_call | solution.py:388
  210.5 8.3 %all_to_all.43 = f32[8,1,128]{2,1,0:T(1,128)S(1)} all-to-all(f32[8,1,128]{2,1,0:T(1,128)S(1)} %broadcast_in_dim.69), channel_id=1, replica_groups=mesh['row_0'=4,'row_1'=2,'cls_0'=4,'cls_1'=8] {'row_0','row_1'}, dimensions={0} | all-to-all | bytes 8192 | tf_op jit(solution)/shard_map/all_to_all | solution.py:71
  218.8 14.2 %all_to_all.44 = f32[8,1,128]{2,1,0:T(1,128)S(1)} all-to-all(f32[8,1,128]{2,1,0:T(1,128)S(1)} %broadcast_in_dim.70), channel_id=1, replica_groups=mesh['row_0'=4,'row_1'=2,'cls_0'=4,'cls_1'=8] {'cls_1'}, dimensions={0} | all-to-all | bytes 8192 | tf_op jit(solution)/shard_map/all_to_all | solution.py:71
  233.0 9.3 %all_to_all.45 = f32[4,1,128]{2,1,0:T(1,128)S(1)} all-to-all(f32[4,1,128]{2,1,0:T(1,128)S(1)} %broadcast_in_dim.71), channel_id=1, replica_groups=mesh['row_0'=4,'row_1'=2,'cls_0'=4,'cls_1'=8] {'cls_0'}, dimensions={0} | all-to-all | bytes 4096 | tf_op jit(solution)/shard_map/all_to_all | solution.py:71
  (65 shorter events, 17.8 us)
Async XLA Ops:
  0.6 33.8 %copy-start = (bf16[2048,512]{1,0:T(8,128)(2,1)S(1)}, bf16[2048,512]{1,0:T(8,128)(2,1)}, u32[]{:S(2)}) copy-start(bf16[2048,512]{1,0:T(8,128)(2,1)} %param.8) | copy-start | bytes 6291460
  0.6 33.1 %copy-start.9 = (s32[1024]{0:T(1024)S(1)}, s32[1024]{0:T(1024)}, u32[]{:S(2)}) copy-start(s32[1024]{0:T(1024)} %param.11) | copy-start | bytes 12292
  0.7 33.7 %copy-start.10 = (s32[1024]{0:T(1024)S(1)}, s32[1024]{0:T(1024)}, u32[]{:S(2)}) copy-start(s32[1024]{0:T(1024)} %param.9) | copy-start | bytes 12292
  33.7 5.8 %copy-start.3 = (bf16[4,8,16,640]{3,2,1,0:T(8,128)(2,1)}, bf16[4,8,16,640]{3,2,1,0:T(8,128)(2,1)S(1)}, u32[]{:S(2)}) copy-start(bf16[4,8,16,640]{3,2,1,0:T(8,128)(2,1)S(1)} %all_to_all.41) | copy-start | bytes 1966084
  33.7 6.4 %collective-permute-start = (bf16[32,16,640]{2,1,0:T(8,128)(2,1)S(1)}, bf16[32,16,640]{2,1,0:T(8,128)(2,1)S(1)}, u32[]{:S(2)}, u32[]{:S(2)}) collective-permute-start(bf16[32,16,640]{2,1,0:T(8,128)(2,1)S(1)} %bitcast.38), channel_id=1, source_target_pairs={{0,32},{32,0},{1,33},{33,1},{2,34},{34,2},{3,35},{35,3},{4,36},{36... | collective-permute-start | bytes 1966088 | tf_op jit(solution)/shard_map/ppermute | solution.py:62
  50.4 1.6 collective-permute-start.1
  63.3 54.7 %copy-start.8 = (f32[8,512]{1,0:T(8,128)}, f32[8,512]{1,0:T(8,128)S(1)}, u32[]{:S(2)}) copy-start(f32[8,512]{1,0:T(8,128)S(1)} %get-tuple-element.39.totals_ref) | copy-start | bytes 49156
  64.1 20.4 %all-to-all-start.3 = ((f32[32,8,512]{2,1,0:T(8,128)}), f32[32,8,512]{2,1,0:T(8,128)S(1)}, u32[]{:S(2)}, u32[]{:S(2)}) async-start(f32[32,8,512]{2,1,0:T(8,128)} %broadcast_in_dim.66), calls=%async_computation.3 | async-start | bytes 1048576 | tf_op jit(solution)/shard_map/all_to_all | solution.py:71
  73.9 19.4 %collective-permute-start.2 = (f32[4,672,128]{2,1,0:T(8,128)}, f32[4,672,128]{2,1,0:T(8,128)}, u32[]{:S(2)}, u32[]{:S(2)}) collective-permute-start(f32[4,672,128]{2,1,0:T(8,128)} %get-tuple-element.24), channel_id=1, source_target_pairs={{0,32},{32,0},{1,33},{33,1},{2,34},{34,2},{3,35},{35,3},{4,36},{36... | collective-permute-start | bytes 4128776 | tf_op jit(solution)/shard_map/ppermute | solution.py:62
  84.6 3.1 %copy-start.7 = (f32[32,8,512]{2,1,0:T(8,128)}, f32[32,8,512]{2,1,0:T(8,128)S(1)}, u32[]{:S(2)}) copy-start(f32[32,8,512]{2,1,0:T(8,128)S(1)} %all-to-all-done.3.own_ref) | copy-start | bytes 1572868
  84.6 1.9 collective-permute-start.10
  86.5 1.1 copy-start.11
  87.6 34.5 %all-to-all-start.4 = ((f32[32,2,8,512]{3,2,1,0:T(8,128)}), f32[32,2,8,512]{3,2,1,0:T(8,128)S(1)}, u32[]{:S(2)}, u32[]{:S(2)}) async-start(f32[32,2,8,512]{3,2,1,0:T(8,128)} %broadcast_in_dim.67), calls=%async_computation.4 | async-start | bytes 2097152 | tf_op jit(solution)/shard_map/all_to_all | solution.py:71
  95.2 12.5 %collective-permute-start.4 = (f32[672,128]{1,0:T(8,128)S(1)}, f32[672,128]{1,0:T(8,128)S(1)}, u32[]{:S(2)}, u32[]{:S(2)}) collective-permute-start(f32[672,128]{1,0:T(8,128)S(1)} %get-tuple-element.35), channel_id=1, source_target_pairs={{0,128},{64,192},{128,0},{192,64},{1,129},{65,193},{129,1},{193,65... | collective-permute-start | bytes 1032200 | tf_op jit(solution)/shard_map/ppermute | solution.py:62
  96.8 16.9 %collective-permute-start.5 = (f32[672,128]{1,0:T(8,128)S(1)}, f32[672,128]{1,0:T(8,128)S(1)}, u32[]{:S(2)}, u32[]{:S(2)}) collective-permute-start(f32[672,128]{1,0:T(8,128)S(1)} %get-tuple-element.36), channel_id=1, source_target_pairs={{0,192},{64,128},{128,64},{192,0},{1,193},{65,129},{129,65},{193,1... | collective-permute-start | bytes 1032200 | tf_op jit(solution)/shard_map/ppermute | solution.py:62
  98.2 15.5 %collective-permute-start.3 = (f32[672,128]{1,0:T(8,128)S(1)}, f32[672,128]{1,0:T(8,128)S(1)}, u32[]{:S(2)}, u32[]{:S(2)}) collective-permute-start(f32[672,128]{1,0:T(8,128)S(1)} %get-tuple-element.37), channel_id=1, source_target_pairs={{0,64},{64,0},{128,192},{192,128},{1,65},{65,1},{129,193},{193,129... | collective-permute-start | bytes 1032200 | tf_op jit(solution)/shard_map/ppermute | solution.py:62
  113.8 17.2 %collective-permute-start.8 = (f32[672,128]{1,0:T(8,128)S(1)}, f32[672,128]{1,0:T(8,128)}, u32[]{:S(2)}, u32[]{:S(2)}) collective-permute-start(f32[672,128]{1,0:T(8,128)S(1)} %bitcast_add_fusion), channel_id=1, source_target_pairs={{0,192},{64,128},{128,64},{192,0},{1,193},{65,129},{129,65},{193,1... | collective-permute-start | bytes 1032200 | tf_op jit(solution)/shard_map/ppermute | solution.py:62
  114.8 16.2 %collective-permute-start.7 = (f32[672,128]{1,0:T(8,128)S(1)}, f32[672,128]{1,0:T(8,128)}, u32[]{:S(2)}, u32[]{:S(2)}) collective-permute-start(f32[672,128]{1,0:T(8,128)S(1)} %bitcast_add_fusion), channel_id=1, source_target_pairs={{0,128},{64,192},{128,0},{192,64},{1,129},{65,193},{129,1},{193,65... | collective-permute-start | bytes 1032200 | tf_op jit(solution)/shard_map/ppermute | solution.py:62
  117.6 15.2 %collective-permute-start.6 = (f32[672,128]{1,0:T(8,128)S(1)}, f32[672,128]{1,0:T(8,128)}, u32[]{:S(2)}, u32[]{:S(2)}) collective-permute-start(f32[672,128]{1,0:T(8,128)S(1)} %bitcast_add_fusion), channel_id=1, source_target_pairs={{0,64},{64,0},{128,192},{192,128},{1,65},{65,1},{129,193},{193,129... | collective-permute-start | bytes 1032200 | tf_op jit(solution)/shard_map/ppermute | solution.py:62
  122.1 12.0 %copy-start.2 = (f32[32,2,8,512]{3,2,1,0:T(8,128)}, f32[32,2,8,512]{3,2,1,0:T(8,128)S(1)}, u32[]{:S(2)}) copy-start(f32[32,2,8,512]{3,2,1,0:T(8,128)S(1)} %all-to-all-done.4.own_ref.cross_own_ref) | copy-start | bytes 3145732
  122.1 43.1 %collective-permute-start.11 = (f32[32,2,8,512]{3,2,1,0:T(8,128)S(1)}, f32[32,2,8,512]{3,2,1,0:T(8,128)S(1)}, u32[]{:S(2)}, u32[]{:S(2)}) collective-permute-start(f32[32,2,8,512]{3,2,1,0:T(8,128)S(1)} %all-to-all-done.4.own_ref.cross_own_ref), channel_id=1, source_target_pairs={{0,32},{32,0},{1,33},{33,1},{2,34},{34,2},{3,35},{35,3},{4,36},{36... | collective-permute-start | bytes 3145736 | tf_op jit(solution)/shard_map/ppermute | solution.py:62
  134.1 31.2 %copy-start.1 = (f32[4,672,128]{2,1,0:T(8,128)}, f32[4,672,128]{2,1,0:T(8,128)S(1)}, u32[]{:S(2)}) copy-start(f32[4,672,128]{2,1,0:T(8,128)S(1)} %pad_maximum_fusion.corr_own_ref) | copy-start | bytes 4128772
  134.1 63.3 %collective-permute-start.9 = (f32[4,672,128]{2,1,0:T(8,128)S(1)}, f32[4,672,128]{2,1,0:T(8,128)S(1)}, u32[]{:S(2)}, u32[]{:S(2)}) collective-permute-start(f32[4,672,128]{2,1,0:T(8,128)S(1)} %pad_maximum_fusion.corr_own_ref), channel_id=1, source_target_pairs={{0,32},{32,0},{1,33},{33,1},{2,34},{34,2},{3,35},{35,3},{4,36},{36... | collective-permute-start | bytes 4128776 | tf_op jit(solution)/shard_map/ppermute | solution.py:62
  197.5 1.1 copy-start.4
  (2 other events, 1.8 us)
